TPU v7x, 512 devices: a whole 4x4x16 slice. The times are simulated.
512 devices in a mesh: sec: 4 (over y), row: 8 (over z_lo), col: 16 (over z_hi, x, core).
Axes of the slice: x: 4, y: 4, z: 16 (z_hi: 2, z_lo: 8; z = z_hi * 8 + z_lo), core: 2. Of those that a mesh axis runs over, the one named last changes fastest.
Arguments:
- rhs: float32 [4, 8192, 256], P('sec', ('row', 'col')), may hold values from -6 to 6
- inv_factor: float32 [4, 8192, 8192], P('sec', 'col', 'row')
- coupling: float32 [4, 8192, 8192], P('sec', 'row', 'col'), may hold values from -0.0625 to 0.0625
- pattern: int32 [4, 64, 64], P('sec', 'row', 'col'), may hold values 0 or 1
Outputs:
- solution: float32 [4, 8192, 256], P('sec', 'col')
- outgoing: float32 [4, 8192, 256], P('sec', ('row', 'col'))
All inputs are finite; a program needn't handle non-finite values. No bound on the sum of `pattern` on one device may be relied on, other than what follows from the above.
Results may differ from a plain program's by a relative error of at most 0.0001.
Values sent between devices are 32-bit elements; how exact they have to be, the bound alone decides.
A program may use at most 64 MiB of HBM per device.

v0:
```python
import jax
import jax.numpy as jnp
from jax import lax
from jax.sharding import PartitionSpec as P


def in_blocks(x, dim, devices):
    before, after = (x.shape[:dim], x.shape[dim + 1 :])
    return jnp.moveaxis(x.reshape(*before, devices, -1, *after), dim, 0)


def sent_and_summed(x, axis, dim):
    parts = in_blocks(x, dim, lax.axis_size(axis))
    arrived = lax.all_to_all(parts, axis, split_axis=0, concat_axis=0, tiled=True)
    return arrived.sum(axis=0)


def sent_to_all(x, axis):
    copies = jnp.broadcast_to(x, (lax.axis_size(axis), *x.shape))
    return lax.all_to_all(copies, axis, split_axis=0, concat_axis=0, tiled=True)


def laid_out(parts, dim):
    dims = list(parts.shape[1:])
    dims[dim] *= parts.shape[0]
    return jnp.moveaxis(parts, 0, dim).reshape(dims)


def gathered_copies(x, axis, dim):
    parts = sent_to_all(x, axis)
    return laid_out(parts, dim)


def over_copies(x, axis):
    everything = sent_to_all(x, axis)
    return jnp.sum(everything, axis=0)


def shards(rhs, inv_factor, coupling, pattern):
    highest = lax.Precision.HIGHEST
    factor = inv_factor[0]
    coupling_local = coupling[0]
    occupancy = pattern[0].astype(jnp.float32)
    block_rows = coupling_local.shape[0] // occupancy.shape[0]
    block_cols = coupling_local.shape[1] // occupancy.shape[1]
    masked = (
        coupling_local.reshape(occupancy.shape[0], block_rows, occupancy.shape[1], block_cols)
        * occupancy[:, None, :, None]
    ).reshape(coupling_local.shape)
    parent_flag = lax.axis_index("sec") == lax.axis_size("sec") - 1
    rows_full = lax.all_gather(rhs[0], "col", axis=0, tiled=True)

    def solve_section(operand):
        shares = sent_and_summed(
            jnp.dot(factor, operand, precision=highest, preferred_element_type=jnp.float32),
            "row",
            0,
        )
        return gathered_copies(shares, "row", 0)

    def run_segment(operand, with_total):
        solved = solve_section(operand)
        update = jnp.dot(masked, solved, precision=highest, preferred_element_type=jnp.float32)
        shares = sent_and_summed(update, "col", 0)
        child_sum = None
        if with_total:
            summed_share = over_copies(jnp.where(parent_flag, 0.0, shares), "sec")
            child_sum = lax.all_gather(summed_share, "col", axis=0, tiled=True)
        return (solved, shares, child_sum)

    solved_a, shares_a, total_a = run_segment(rows_full, True)
    solved_b, shares_b, unused = run_segment(rows_full - total_a, False)
    solution = jnp.where(parent_flag, solved_b, solved_a)
    outgoing = jnp.where(parent_flag, shares_b, shares_a)
    return (solution[None], outgoing[None])


def solution(mesh):
    placed = (
        P("sec", ("row", "col"), None),
        P("sec", "col", "row"),
        P("sec", "row", "col"),
        P("sec", "row", "col"),
    )
    return jax.shard_map(
        shards,
        mesh=mesh,
        in_specs=placed,
        out_specs=(P("sec", "col", None), P("sec", ("row", "col"), None)),
        check_vma=False,
    )
```

profile of v0, /device:TPU:24, one launch (start us, length us, event | category | flops | bytes accessed | tf_op | source)
XLA Modules:
  0.0 459.3 jit_solution(11764051076981974164)
XLA Ops:
  7.2 0.0 copy-start
  7.2 0.0 all-gather.6.cloned.1.call-start
  7.2 0.7 all-gather.6.cloned.1.call-update
  7.9 85.3 %all-gather.6.cloned.1.call-done = f32[1,1024,256]{2,1,0:T(8,128)} async-done(((f32[1,64,256]{2,1,0:T(8,128)}), f32[1,1024,256]{2,1,0:T(8,128)}) %all-gather.6.cloned.1.call-update) | async-done | bytes 1048592 | tf_op jit(solution)/shard_map/all_gather | solution.py:51
  93.2 0.0 copy-done
  93.2 3.0 fusion.5
  96.3 0.0 copy-start.1
  96.3 31.8 %all_to_all.35 = f32[8,64,256]{2,1,0:T(8,128)S(1)} all-to-all(f32[8,64,256]{2,1,0:T(8,128)S(1)} %fusion.5), channel_id=1, replica_groups=mesh['sec'=4,'row'=8,'col'=16] {'row'}, dimensions={0} | all-to-all | bytes 1048576 | tf_op jit(solution)/shard_map/all_to_all | solution.py:14
  128.1 0.8 broadcast_in_dim.17
  129.0 4.3 all-to-all-start.1
  133.2 0.0 copy-done.1
  133.3 0.1 copy.9
  133.3 1.7 mul.17
  135.0 3.1 mul.18
  138.1 4.0 mul.19
  142.1 19.8 %all-to-all-done.1 = f32[8,64,256]{2,1,0:T(8,128)S(1)} async-done(((f32[8,64,256]{2,1,0:T(8,128)}), f32[8,64,256]{2,1,0:T(8,128)S(1)}, u32[]{:S(2)}, u32[]{:S(2)}) %all-to-all-start.1) | async-done | bytes 524320 | tf_op jit(solution)/shard_map/all_to_all | solution.py:20
  161.9 4.4 fusion.7
  166.4 9.2 %all-to-all-start.2 = ((f32[16,64,256]{2,1,0:T(8,128)}), f32[16,64,256]{2,1,0:T(8,128)}, u32[]{:S(2)}, u32[]{:S(2)}) async-start(f32[16,64,256]{2,1,0:T(8,128)} %fusion.7), calls=%async_computation.2 | async-start | bytes 2097152 | tf_op jit(solution)/shard_map/all_to_all | solution.py:14
  175.5 0.0 all-gather.4.cloned.1.call-start
  175.6 47.1 %all-to-all-done.2 = f32[16,64,256]{2,1,0:T(8,128)} async-done(((f32[16,64,256]{2,1,0:T(8,128)}), f32[16,64,256]{2,1,0:T(8,128)}, u32[]{:S(2)}, u32[]{:S(2)}) %all-to-all-start.2) | async-done | bytes 1048608 | tf_op jit(solution)/shard_map/all_to_all | solution.py:14
  222.7 1.3 reduce_sum.46
  224.0 9.2 %all_to_all.36 = f32[4,64,256]{2,1,0:T(8,128)S(1)} all-to-all(f32[4,64,256]{2,1,0:T(8,128)S(1)} %broadcast_in_dim.18), channel_id=1, replica_groups=mesh['sec'=4,'row'=8,'col'=16] {'sec'}, dimensions={0} | all-to-all | bytes 524288 | tf_op jit(solution)/shard_map/all_to_all | solution.py:20
  233.2 0.6 reduce_sum.47
  233.8 0.0 all-gather.4.cloned.1.call-update
  233.9 79.5 %all-gather.4.cloned.1.call-done = f32[1024,256]{1,0:T(8,128)} async-done(((f32[64,256]{1,0:T(8,128)}), f32[1024,256]{1,0:T(8,128)}) %all-gather.4.cloned.1.call-update) | async-done | bytes 1048592 | tf_op jit(solution)/shard_map/all_gather | solution.py:68
  313.4 5.1 %fusion.2 = f32[512,256]{0,1:T(8,128)S(1)} fusion(f32[1,512,1024]{2,1,0:T(8,128)S(1)} %copy-done, f32[1024,256]{1,0:T(8,128)} %all-gather.4.cloned.1.call-done, f32[1,1024,256]{2,1,0:T(8,128)} %all-gather.6.cloned.1.call-done), kind=kOutput, calls=%fused_computation.2 | convolution fusion | flops 1610874880 | bytes 4718592 | tf_op jit(solution)/shard_map/dot_general | solution.py:55
  318.5 1.0 copy.10
  319.5 32.8 %all_to_all.37 = f32[8,64,256]{2,1,0:T(8,128)S(1)} all-to-all(f32[8,64,256]{2,1,0:T(8,128)} %bitcast.37), channel_id=1, replica_groups=mesh['sec'=4,'row'=8,'col'=16] {'row'}, dimensions={0} | all-to-all | bytes 1048576 | tf_op jit(solution)/shard_map/all_to_all | solution.py:14
  352.4 32.8 %all_to_all.38 = f32[8,64,256]{2,1,0:T(8,128)S(1)} all-to-all(f32[8,64,256]{2,1,0:T(8,128)S(1)} %broadcast_in_dim.19), channel_id=1, replica_groups=mesh['sec'=4,'row'=8,'col'=16] {'row'}, dimensions={0} | all-to-all | bytes 1048576 | tf_op jit(solution)/shard_map/all_to_all | solution.py:20
  385.1 4.4 fusion.8
  389.5 8.4 %all-to-all-start.6 = ((f32[16,64,256]{2,1,0:T(8,128)}), f32[16,64,256]{2,1,0:T(8,128)}, u32[]{:S(2)}, u32[]{:S(2)}) async-start(f32[16,64,256]{2,1,0:T(8,128)} %fusion.8), calls=%async_computation.6 | async-start | bytes 2097152 | tf_op jit(solution)/shard_map/all_to_all | solution.py:14
  397.9 0.9 broadcast_select_fusion
  398.8 51.8 %all-to-all-done.6 = f32[16,64,256]{2,1,0:T(8,128)} async-done(((f32[16,64,256]{2,1,0:T(8,128)}), f32[16,64,256]{2,1,0:T(8,128)}, u32[]{:S(2)}, u32[]{:S(2)}) %all-to-all-start.6) | async-done | bytes 1048608 | tf_op jit(solution)/shard_map/all_to_all | solution.py:14
  450.6 1.3 reduce_sum.49
  451.9 0.6 select_bitcast_fusion
  (6 shorter events, 0.1 us)
Async XLA Ops:
  7.2 86.1 %copy-start = (f32[1,512,1024]{2,1,0:T(8,128)S(1)}, f32[1,512,1024]{2,1,0:T(8,128)}, u32[]{:S(2)}) copy-start(f32[1,512,1024]{2,1,0:T(8,128)} %param.5) | copy-start | bytes 6291460
  7.2 86.1 %all-gather.6.cloned.1.call-start = ((), (), s32[]{:S(2)}) async-start(), calls=%async_computation.8 | async-start | bytes 1114112 | tf_op jit(solution)/shard_map/all_gather | solution.py:51
  96.3 37.0 %copy-start.1 = (s32[1,8,4]{1,2,0:T(4,128)S(1)}, s32[1,8,4]{1,2,0:T(4,128)}, u32[]{:S(2)}) copy-start(s32[1,8,4]{1,2,0:T(4,128)} %param.7) | copy-start | bytes 388
  129.0 33.0 %all-to-all-start.1 = ((f32[8,64,256]{2,1,0:T(8,128)}), f32[8,64,256]{2,1,0:T(8,128)S(1)}, u32[]{:S(2)}, u32[]{:S(2)}) async-start(f32[8,64,256]{2,1,0:T(8,128)} %broadcast_in_dim.17), calls=%async_computation.1 | async-start | bytes 1048576 | tf_op jit(solution)/shard_map/all_to_all | solution.py:20
  166.4 56.3 %all-to-all-start.2 = ((f32[16,64,256]{2,1,0:T(8,128)}), f32[16,64,256]{2,1,0:T(8,128)}, u32[]{:S(2)}, u32[]{:S(2)}) async-start(f32[16,64,256]{2,1,0:T(8,128)} %fusion.7), calls=%async_computation.2 | async-start | bytes 2097152 | tf_op jit(solution)/shard_map/all_to_all | solution.py:14
  175.5 137.9 %all-gather.4.cloned.1.call-start = ((), (), s32[]{:S(2)}) async-start(), calls=%async_computation.7 | async-start | bytes 1114112 | tf_op jit(solution)/shard_map/all_gather | solution.py:68
  389.5 61.1 %all-to-all-start.6 = ((f32[16,64,256]{2,1,0:T(8,128)}), f32[16,64,256]{2,1,0:T(8,128)}, u32[]{:S(2)}, u32[]{:S(2)}) async-start(f32[16,64,256]{2,1,0:T(8,128)} %fusion.8), calls=%async_computation.6 | async-start | bytes 2097152 | tf_op jit(solution)/shard_map/all_to_all | solution.py:14
Sparse Core Ops, SparseCore 0:
  11.3 81.8 all-gather.5
  234.0 79.3 all-gather.3
where the time goes:
time: 464 us; the launch traced here: 459 us
  waiting for transfers between devices  284 us (61%)
  blocking collectives  107 us (23%)
  starting transfers between devices  21.9 us (5%)
  matrix products  16.9 us (4%)
  between operations  14.1 us (3%)
  other arithmetic  8.81 us (2%)
  local copies, waits for them, and re-layouts  6.74 us (1%)
    all_to_all x2, waiting for transfers between devices, sent_and_summed(): lax.all_to_all(parts, axis, split_axis=0, concat_axis=0, tiled=True)  98.9 us
    all_gather x1, waiting for transfers between devices, shards(): rows_full = lax.all_gather(rhs[0], 'col', axis=0, tiled=True)  85.3 us
    all_gather x1, waiting for transfers between devices, run_segment(): child_sum = lax.all_gather(summed_share, 'col', axis=0, tiled=True)  79.5 us
    all_to_all x2, blocking collectives, sent_and_summed(): lax.all_to_all(parts, axis, split_axis=0, concat_axis=0, tiled=True)  64.6 us
    all_to_all x2, blocking collectives, sent_to_all(): return lax.all_to_all(copies, axis, split_axis=0, concat_axis=0, tiled=True)  41.9 us
    all_to_all x1, waiting for transfers between devices, sent_to_all(): return lax.all_to_all(copies, axis, split_axis=0, concat_axis=0, tiled=True)  19.8 us
    all_to_all x2, starting transfers between devices, sent_and_summed(): lax.all_to_all(parts, axis, split_axis=0, concat_axis=0, tiled=True)  17.5 us
  transfers between devices with their start and end apart: 5, of which 5 were waited for; matrix products, arithmetic and copies ran while one was open for 2% of the time, Pallas kernels for 0%

commit v1 on v0

v1 whole, which is shorter than its diff:
```python
import jax
import jax.numpy as jnp
from jax import lax
from jax.experimental import pallas as pl
from jax.experimental.pallas import tpu as pltpu
from jax.sharding import PartitionSpec as P

MESH = pl.DeviceIdType.MESH
F32 = jnp.float32
BF16 = jnp.bfloat16
CHUNK = 32
CHUNKS = 512 // CHUNK
LAG = 5


def split(v):
    high = v.astype(BF16)
    return high, (v - high.astype(F32)).astype(BF16)


def dot3(ah, al, bh, bl):
    low = jnp.dot(al, bh, preferred_element_type=F32) + jnp.dot(ah, bl, preferred_element_type=F32)
    return jnp.dot(ah, bh, preferred_element_type=F32) + low


def kernel(
    rhs, inv_hbm, cpl_hbm, pat, sol, out,
    inv_v, cpl_v, ah, al, ch, cl, xg, xh, xl, part, inb, bk, yh, yl,
    ub, cb, vb, rb, wb, pb, qb, qr, zb, ob,
    load_sem, store_sem, z0s, z0r, axs, axr, acs, acr, fs, fr, bs, br,
    cs, cr, rs, rr, ys, yr, qs, qrs, zs, zr,
):
    s, r, c = lax.axis_index("sec"), lax.axis_index("row"), lax.axis_index("col")
    zh, x, k = c // 8, (c // 2) % 4, c % 2
    is_parent = s == 3
    depth = jnp.where(r < 4, r, 7 - r)
    inward = jnp.where(r < 4, r + 1, r - 1)
    outward = jnp.clip(jnp.where(r < 4, r - 1, r + 1), 0, 7)

    def at(zz, xx, kk):
        return {"col": zz * 8 + xx * 2 + kk}

    core = at(zh, x, 1 - k)
    far = at(1 - zh, x, k)
    ring = {d: at(zh, (x + d) % 4, k) for d in (1, 2, 3)}

    def remote(src, dst, send, recv, device):
        return pltpu.make_async_remote_copy(
            src_ref=src, dst_ref=dst, send_sem=send, recv_sem=recv, device_id=device, device_id_type=MESH
        )

    load_inv = pltpu.make_async_copy(inv_hbm, inv_v, load_sem.at[0])
    load_cpl = pltpu.make_async_copy(cpl_hbm, cpl_v, load_sem.at[1])
    load_inv.start()
    load_cpl.start()

    barrier = pltpu.get_barrier_semaphore()

    def greet(device):
        pl.semaphore_signal(barrier, inc=1, device_id=device, device_id_type=MESH)

    for device in (core, far, ring[1], ring[2], ring[3], {"row": inward}):
        greet(device)

    @pl.when(depth > 0)
    def _():
        greet({"row": outward})

    @pl.when(is_parent)
    def _():
        for child in range(3):
            greet({"sec": child})

    @pl.when(jnp.logical_not(is_parent))
    def _():
        greet({"sec": 3})

    pl.semaphore_wait(barrier, 7 + jnp.where(depth > 0, 1, 0) + jnp.where(is_parent, 2, 0))

    def gather_copy(zz, d, src):
        return remote(src, xg.at[zz, x, k], axs.at[zz, d - 1], axr.at[zz, d - 1], ring[d])

    def core_copy(zz, d, src):
        return remote(src, xg.at[zz, (x + 4 - d) % 4, k], acs.at[zz, d], acr.at[zz, d], core)

    def gather_send(zz, src):
        for d in (2, 1, 3):
            gather_copy(zz, d, src).start()
        core_copy(zz, 0, src).start()

    def gather_forward(zz):
        for d in (1, 3, 2):
            piece = xg.at[zz, (x + 4 - d) % 4, k]
            gather_copy(zz, d, piece).wait_recv()
            core_copy(zz, d, piece).start()

    def z0():
        return remote(rhs, xg.at[zh, x, k], z0s, z0r, far)

    @pl.when(jnp.logical_not(is_parent))
    def _():
        z0().start()
        gather_send(zh, rhs)
        xg[zh, x, k] = rhs[...]

    load_inv.wait()

    def split_inv(i, carry):
        rows = pl.ds(pl.multiple_of(i * 64, 64), 64)
        ah[rows, :], al[rows, :] = split(inv_v[rows, :])
        return carry

    lax.fori_loop(0, 8, split_inv, 0)
    load_cpl.wait()

    def split_cpl(i, carry):
        rows = pl.ds(pl.multiple_of(i * 128, 128), 128)
        to = pl.ds(pl.multiple_of((lax.rem(i, 4) * 2 + i // 4) * 128, 128), 128)
        for j in range(4):
            cols = pl.ds(j * 128, 128)
            ch[to, cols], cl[to, cols] = split(cpl_v[rows, cols] * pat[i, j].astype(F32))
        return carry

    lax.fori_loop(0, 8, split_cpl, 0)

    @pl.when(jnp.logical_not(is_parent))
    def _():
        gather_forward(zh)
        z0().wait_recv()
        gather_send(1 - zh, xg.at[1 - zh, x, k])
        gather_forward(1 - zh)
        z0().wait_send()

    def to_parent(slot):
        return remote(wb, pb.at[slot], ys, yr.at[slot], {"sec": 3})

    def q_copy():
        return remote(qb, qr, qs, qrs, far)

    @pl.when(is_parent)
    def _():
        for child in range(3):
            to_parent(child).wait_recv()
        qb[zh] = rhs[...] - (pb[0, zh] + pb[1, zh] + pb[2, zh])
        qb[1 - zh] = -(pb[0, 1 - zh] + pb[1, 1 - zh] + pb[2, 1 - zh])
        q_copy().start()
        q_copy().wait_recv()
        for zz in range(2):
            xg[zz, x, k] = qb[zz] + qr[zz]
            gather_send(zz, xg.at[zz, x, k])
        for zz in range(2):
            gather_forward(zz)
        q_copy().wait_send()

    for zz in range(2):
        for d in range(4):
            core_copy(zz, d, xg.at[zz, x, k]).wait_recv()

    for zz in range(2):
        for xx in range(4):
            for kk in range(2):
                rows = pl.ds((zz * 8 + xx * 2 + kk) * 64, 64)
                xh[rows, :], xl[rows, :] = split(xg[zz, xx, kk])

    def solve(i, carry):
        rows = pl.ds(pl.multiple_of(i * 256, 256), 256)
        part[rows, :] = dot3(ah[rows, :], al[rows, :], xh[...], xl[...])
        return carry

    lax.fori_loop(0, 2, solve, 0)

    def rows_of(m):
        return pl.ds(pl.multiple_of(m * CHUNK, CHUNK), CHUNK)

    def in_copy(m):
        return remote(part.at[rows_of(m)], inb.at[rows_of(m)], fs.at[m], fr.at[m], {"row": inward})

    def across_copy(m):
        return remote(part.at[rows_of(m)], bk.at[rows_of(m)], fs.at[m], br.at[m], {"row": inward})

    def out_copy(m):
        return remote(bk.at[rows_of(m)], bk.at[rows_of(m)], bs.at[m], br.at[m], {"row": outward})

    def forward(m):
        @pl.when(depth > 0)
        def _():
            in_copy(m).wait_recv()
            part[rows_of(m), :] = part[rows_of(m), :] + inb[rows_of(m), :]

        @pl.when(depth < 3)
        def _():
            in_copy(m).start()

        @pl.when(depth == 3)
        def _():
            across_copy(m).start()

    def back(m):
        across_copy(m).wait_recv()

        @pl.when(depth == 3)
        def _():
            bk[rows_of(m), :] = part[rows_of(m), :] + bk[rows_of(m), :]

        @pl.when(depth > 0)
        def _():
            out_copy(m).start()

    lag = jnp.where(depth == 3, LAG, CHUNKS)

    def both(i, carry):
        @pl.when(i < CHUNKS)
        def _():
            forward(i)

        @pl.when(jnp.logical_and(i >= lag, i - lag < CHUNKS))
        def _():
            back(i - lag)

        return carry

    lax.fori_loop(0, CHUNKS + lag, both, 0)

    store = pltpu.make_async_copy(bk, sol, store_sem.at[0])
    store.start()
    yh[...], yl[...] = split(bk[...])

    def pair_copy(d):
        xx = (x + d) % 4
        return remote(ub.at[1 - k, xx], cb.at[xx], cs.at[d], cr.at[d], core)

    def pair_copy_in(d):
        return pair_copy(d)

    def sum_copy(d):
        return remote(vb.at[d - 1], rb.at[d - 1], rs.at[d - 1], rr.at[d - 1], ring[d])

    order = (2, 1, 3, 0)
    for d in order:
        xx = (x + d) % 4
        rows = pl.ds(pl.multiple_of(xx * 256, 256), 256)
        u = dot3(ch[rows, :], cl[rows, :], yh[...], yl[...])
        for zz in range(2):
            for kk in range(2):
                at_row = (zz * 2 + kk) * 64
                ub[kk, xx, zz] = u[at_row : at_row + 64]
        pair_copy(d).start()
    for d in order[:3]:
        xx = (x + d) % 4
        pair_copy_in(d).wait_recv()
        vb[d - 1] = ub[k, xx] + cb[xx]
        sum_copy(d).start()
    pair_copy_in(0).wait_recv()
    own = ub[k, x] + cb[x]
    for d in (1, 3, 2):
        sum_copy(d).wait_recv()
    wb[...] = own + (rb[0] + rb[1] + rb[2])

    @pl.when(jnp.logical_not(is_parent))
    def _():
        to_parent(s).start()

    z_copy = remote(wb.at[1 - zh], zb, zs, zr, far)
    z_copy.start()
    z_copy.wait_recv()
    ob[...] = wb[zh] + zb[...]
    store_out = pltpu.make_async_copy(ob, out, store_sem.at[1])
    store_out.start()

    z_copy.wait_send()

    @pl.when(jnp.logical_not(is_parent))
    def _():
        to_parent(s).wait_send()

    for d in (1, 2, 3):
        sum_copy(d).wait_send()
    for d in range(4):
        pair_copy(d).wait_send()
    for zz in range(2):
        for d in (1, 2, 3):
            gather_copy(zz, d, xg.at[zz, x, k]).wait_send()
        for d in range(4):
            core_copy(zz, d, xg.at[zz, x, k]).wait_send()

    def drain(m, carry):
        in_copy(m).wait_send()

        @pl.when(depth > 0)
        def _():
            out_copy(m).wait_send()

        return carry

    lax.fori_loop(0, CHUNKS, drain, 0)
    store.wait()
    store_out.wait()


def shards(rhs, inv_factor, coupling, pattern):
    dma = pltpu.SemaphoreType.DMA
    vmem = pltpu.VMEM
    any_space = pl.BlockSpec(memory_space=pl.ANY)
    solved, sent = pl.pallas_call(
        kernel,
        out_shape=(jax.ShapeDtypeStruct((512, 256), F32), jax.ShapeDtypeStruct((64, 256), F32)),
        in_specs=[
            pl.BlockSpec(memory_space=pltpu.VMEM),
            any_space,
            any_space,
            pl.BlockSpec(memory_space=pltpu.SMEM),
        ],
        out_specs=(any_space, any_space),
        scratch_shapes=[
            vmem((512, 1024), F32), vmem((1024, 512), F32),
            vmem((512, 1024), BF16), vmem((512, 1024), BF16),
            vmem((1024, 512), BF16), vmem((1024, 512), BF16),
            vmem((2, 4, 2, 64, 256), F32),
            vmem((1024, 256), BF16), vmem((1024, 256), BF16),
            vmem((512, 256), F32), vmem((512, 256), F32), vmem((512, 256), F32),
            vmem((512, 256), BF16), vmem((512, 256), BF16),
            vmem((2, 4, 2, 64, 256), F32), vmem((4, 2, 64, 256), F32),
            vmem((3, 2, 64, 256), F32), vmem((3, 2, 64, 256), F32),
            vmem((2, 64, 256), F32),
            vmem((3, 2, 64, 256), F32),
            vmem((2, 64, 256), F32), vmem((2, 64, 256), F32),
            vmem((64, 256), F32), vmem((64, 256), F32),
            dma((2,)), dma((2,)), dma, dma,
            dma((2, 3)), dma((2, 3)), dma((2, 4)), dma((2, 4)),
            dma((CHUNKS,)), dma((CHUNKS,)), dma((CHUNKS,)), dma((CHUNKS,)),
            dma((4,)), dma((4,)), dma((3,)), dma((3,)),
            dma, dma((3,)), dma, dma, dma, dma,
        ],
        compiler_params=pltpu.CompilerParams(
            collective_id=0, has_side_effects=True, vmem_limit_bytes=40 * 1024 * 1024
        ),
        name="eliminate",
    )(rhs[0], inv_factor[0], coupling[0], pattern[0])
    return solved[None], sent[None]


def solution(mesh):
    placed = (
        P("sec", ("row", "col"), None),
        P("sec", "col", "row"),
        P("sec", "row", "col"),
        P("sec", "row", "col"),
    )
    return jax.shard_map(
        shards,
        mesh=mesh,
        in_specs=placed,
        out_specs=(P("sec", "col", None), P("sec", ("row", "col"), None)),
        check_vma=False,
    )
```

time: 464 us -> 160 us (0.34)
  waiting for transfers between devices: 284 us -> 0 us
  Pallas kernels: 0 us -> 153 us
  blocking collectives: 107 us -> 0 us
  starting transfers between devices: 21.9 us -> 0 us
  matrix products: 16.9 us -> 0 us
  between operations: 14.1 us -> 0.64 us
  other arithmetic: 8.81 us -> 0 us
    all_gather x2 -> x0, waiting for transfers between devices: 165 us -> none  [the longest x1 85.3 us: shards(): rows_full = lax.all_gather(rhs[0], 'col', axis=0, tiled=True)]
    pallas_call x0 -> x1, Pallas kernels: none -> 153 us  [shards(): pl.pallas_call(kernel, out_shape=(jax.ShapeDtypeStruct((512, 256), F32),...]
    all_to_all x3 -> x0, waiting for transfers between devices: 119 us -> none  [the longest x2 98.9 us: sent_and_summed(): lax.all_to_all(parts, axis, split_axis=0, concat_axis=0, tiled=True)]
    all_to_all x4 -> x0, blocking collectives: 107 us -> none  [the longest x2 64.6 us: sent_and_summed(): lax.all_to_all(parts, axis, split_axis=0, concat_axis=0, tiled=True)]
    all_to_all x3 -> x0, starting transfers between devices: 21.8 us -> none  [the longest x2 17.5 us: sent_and_summed(): lax.all_to_all(parts, axis, split_axis=0, concat_axis=0, tiled=True)]
    dot_general x4 -> x0, matrix products: 16.9 us -> none  [the longest x2 8.79 us: run_segment(): jnp.dot(masked, solved, precision=highest, preferred_element_type=jnp.flo...]
    unnamed x4 -> x8, local copies, waits for them, and re-layouts: 0.02 us -> 5.44 us
    mul x2 -> x0, local copies, waits for them, and re-layouts: 4.75 us -> none  [shards(): coupling_local.reshape(occupancy.shape[0], block_rows, occupancy.shape[1]...]
  transfers between devices with their start and end apart: 5 -> 0, of which waited for: 5 -> 0; matrix products, arithmetic and copies ran while one was open for 2% -> 0% of each run, Pallas kernels for 0% -> 0%
where the time goes in v1:
time: 160 us
  Pallas kernels  153 us (96%)
  local copies, waits for them, and re-layouts  6.2 us (4%)
    pallas_call x1, Pallas kernels, shards(): pl.pallas_call(kernel, out_shape=(jax.ShapeDtypeStruct((512, 256), F32),...  153 us
    unnamed x8, local copies, waits for them, and re-layouts  5.44 us

profile of v1, /device:TPU:24, one launch (start us, length us, event | category | flops | bytes accessed | tf_op | source)
XLA Modules:
  0.0 160.0 jit_solution(18006800865369350254)
XLA Ops:
  0.6 0.8 copy.6.pat
  1.4 0.0 copy-start
  1.4 1.6 copy-done
  3.0 0.0 copy-start.1
  3.0 1.6 copy-done.1
  4.6 0.0 copy-start.2
  4.6 0.8 copy-done.2
  5.4 153.1 %eliminate.1 = (f32[512,256]{1,0:T(8,128)S(1)}, f32[64,256]{1,0:T(8,128)S(1)}) custom-call(f32[64,256]{1,0:T(8,128)S(1)} %bitcast.9, f32[512,1024]{1,0:T(8,128)S(1)} %bitcast.6, f32[1024,512]{1,0:T(8,128)S(1)} %bitcast.7, s32[8,4]{1,0:T(8,128)S(1)} %copy.6.pat), custom_call_target="tpu_custom_call" | custom-call | tf_op jit(solution)/shard_map/eliminate/pallas_call | solution.py:304
  158.6 0.8 copy.9
  159.4 0.6 copy.10
Async XLA Ops:
  1.4 1.6 copy-start
  3.0 1.6 copy-start.1
  4.6 0.8 copy-start.2

commit v2 on v1

v2 whole, which is shorter than its diff:
```python
import jax
import jax.numpy as jnp
from jax import lax
from jax.experimental import pallas as pl
from jax.experimental.pallas import tpu as pltpu
from jax.sharding import PartitionSpec as P

MESH = pl.DeviceIdType.MESH
F32 = jnp.float32
BF16 = jnp.bfloat16
HALF = 128
CHUNK = 32
PER = 512 // CHUNK
CHUNKS = 2 * PER
LAGS = (0, CHUNKS, (3 * CHUNKS) // 4, CHUNKS // 4)
SENT = PER + PER // 2


def split(v):
    high = v.astype(BF16)
    return high, (v - high.astype(F32)).astype(BF16)


def product(ah, al, b):
    wide = jnp.dot(ah, b, preferred_element_type=F32)
    low = jnp.dot(al, b[:, :HALF], preferred_element_type=F32)
    return wide[:, :HALF] + (wide[:, HALF:] + low)


def kernel(
    rhs, inv_hbm, cpl_hbm, pat, sol, out,
    inv_v, cpl_v, ah, al, ch, cl, xg, xs, part, inb, bk, yv,
    ub, cb, vb, rb, wb, pb, qb, qr, zb, ob,
    load_sem, store_sem, z0s, z0r, axs, axr, acs, acr, fs, fr, bs, br,
    cs, cr, rs, rr, ys, yr, qs, qrs, zs, zr,
):
    s, r, c = lax.axis_index("sec"), lax.axis_index("row"), lax.axis_index("col")
    zh, x, k = c // 8, (c // 2) % 4, c % 2
    is_parent = s == 3
    is_child = s < 3
    depth = jnp.where(r < 4, r, 7 - r)
    inward = jnp.where(r < 4, r + 1, r - 1)
    outward = jnp.clip(jnp.where(r < 4, r - 1, r + 1), 0, 7)

    def at(zz, xx, kk):
        return {"col": zz * 8 + xx * 2 + kk}

    core = at(zh, x, 1 - k)
    far = at(1 - zh, x, k)
    ring = {d: at(zh, (x + d) % 4, k) for d in (1, 2, 3)}

    def remote(src, dst, send, recv, device):
        return pltpu.make_async_remote_copy(
            src_ref=src, dst_ref=dst, send_sem=send, recv_sem=recv, device_id=device, device_id_type=MESH
        )

    load_inv = pltpu.make_async_copy(inv_hbm, inv_v, load_sem.at[0])
    load_cpl = pltpu.make_async_copy(cpl_hbm, cpl_v, load_sem.at[1])
    load_inv.start()
    load_cpl.start()

    barrier = pltpu.get_barrier_semaphore()

    def greet(device):
        pl.semaphore_signal(barrier, inc=1, device_id=device, device_id_type=MESH)

    for device in (far, ring[2], ring[1], ring[3], {"row": inward}, core):
        greet(device)

    @pl.when(depth > 0)
    def _():
        greet({"row": outward})

    @pl.when(is_parent)
    def _():
        for child in range(3):
            greet({"sec": child})

    @pl.when(is_child)
    def _():
        greet({"sec": 3})

    load_inv.wait()

    def split_inv(i, carry):
        rows = pl.ds(pl.multiple_of(i * 64, 64), 64)
        ah[rows, :], al[rows, :] = split(inv_v[rows, :])
        return carry

    lax.fori_loop(0, 8, split_inv, 0)
    load_cpl.wait()

    def split_cpl(i, carry):
        rows = pl.ds(pl.multiple_of(i * 128, 128), 128)
        to = pl.ds(pl.multiple_of((lax.rem(i, 4) * 2 + i // 4) * 128, 128), 128)
        for j in range(4):
            cols = pl.ds(j * 128, 128)
            ch[to, cols], cl[to, cols] = split(cpl_v[rows, cols] * pat[j, i].astype(F32))
        return carry

    lax.fori_loop(0, 8, split_cpl, 0)

    pl.semaphore_wait(barrier, 7 + jnp.where(depth > 0, 1, 0) + jnp.where(is_parent, 2, 0))

    def half(h):
        return pl.ds(h * HALF, HALF)

    def gather_copy(h, zz, d, src):
        return remote(src, xg.at[h, zz, x, k], axs.at[h, zz, d - 1], axr.at[h, zz, d - 1], ring[d])

    def core_copy(h, zz, d, src):
        return remote(src, xg.at[h, zz, (x + 4 - d) % 4, k], acs.at[h, zz, d], acr.at[h, zz, d], core)

    def gather_send(h, zz, src):
        for d in (2, 1, 3):
            gather_copy(h, zz, d, src).start()
        core_copy(h, zz, 0, src).start()

    def gather_forward(h, zz):
        for d in (1, 3, 2):
            piece = xg.at[h, zz, (x + 4 - d) % 4, k]
            gather_copy(h, zz, d, piece).wait_recv()
            core_copy(h, zz, d, piece).start()

    def z0(h):
        return remote(rhs.at[:, half(h)], xg.at[h, zh, x, k], z0s.at[h], z0r.at[h], far)

    def to_parent(h, slot):
        return remote(wb.at[h], pb.at[h, slot], ys.at[h], yr.at[h, slot], {"sec": 3})

    def q_copy(h, zz):
        return remote(qb.at[h, zz], qr.at[h, zz], qs.at[h, zz], qrs.at[h, zz], far)

    def q_send(h):
        for child in range(3):
            to_parent(h, child).wait_recv()
        for zz in range(2):
            mine = jnp.where(zh == zz, rhs[:, half(h)], 0.0)
            qb[h, zz] = mine - (pb[h, 0, zz] + pb[h, 1, zz] + pb[h, 2, zz])
            q_copy(h, zz).start()

    def q_arrive(h, zz):
        q_copy(h, zz).wait_recv()
        xg[h, zz, x, k] = qb[h, zz] + qr[h, zz]
        gather_send(h, zz, xg.at[h, zz, x, k])

    @pl.when(is_child)
    def _():
        for h in range(2):
            z0(h).start()
        for h in range(2):
            gather_send(h, zh, rhs.at[:, half(h)])
            xg[h, zh, x, k] = rhs[:, half(h)]
        for h in range(2):
            gather_forward(h, zh)
        for h in range(2):
            z0(h).wait_recv()
            gather_send(h, 1 - zh, xg.at[h, 1 - zh, x, k])
        gather_forward(0, 1 - zh)

    @pl.when(is_parent)
    def _():
        q_send(0)
        q_send(1)
        q_arrive(0, 0)
        q_arrive(0, 1)
        q_arrive(1, 0)
        gather_forward(0, 0)
        gather_forward(0, 1)

    def rows_of(m):
        return pl.ds(pl.multiple_of(m * CHUNK, CHUNK), CHUNK)

    def in_copy(m):
        return remote(part.at[rows_of(m)], inb.at[rows_of(m)], fs.at[m], fr.at[m], {"row": inward})

    def across_copy(m):
        return remote(part.at[rows_of(m)], bk.at[rows_of(m)], fs.at[m], br.at[m], {"row": inward})

    def out_copy(m):
        return remote(bk.at[rows_of(m)], bk.at[rows_of(m)], bs.at[m], br.at[m], {"row": outward})

    def solve(h):
        for zz in range(2):
            for d in range(4):
                core_copy(h, zz, d, xg.at[h, zz, x, k]).wait_recv()
        for zz in range(2):
            for xx in range(4):
                for kk in range(2):
                    rows = pl.ds((zz * 8 + xx * 2 + kk) * 64, 64)
                    xs[h, rows, :HALF], xs[h, rows, HALF:] = split(xg[h, zz, xx, kk])
        for i in range(2):
            rows = pl.ds(i * 256, 256)
            part[pl.ds(h * 512 + i * 256, 256), :] = product(ah[rows, :], al[rows, :], xs[h])

        @pl.when(depth == 0)
        def _():
            def send(m, carry):
                in_copy(m).start()
                return carry

            lax.fori_loop(h * PER, (h + 1) * PER, send, 0)

    solve(0)

    @pl.when(is_child)
    def _():
        gather_forward(1, 1 - zh)

    @pl.when(is_parent)
    def _():
        q_arrive(1, 1)
        gather_forward(1, 0)
        gather_forward(1, 1)

    solve(1)

    def forward(m):
        in_copy(m).wait_recv()
        part[rows_of(m), :] = part[rows_of(m), :] + inb[rows_of(m), :]

        @pl.when(depth < 3)
        def _():
            in_copy(m).start()

        @pl.when(depth == 3)
        def _():
            across_copy(m).start()

    def back(m):
        across_copy(m).wait_recv()

        @pl.when(depth == 3)
        def _():
            bk[rows_of(m), :] = part[rows_of(m), :] + bk[rows_of(m), :]

        @pl.when(depth > 0)
        def _():
            out_copy(m).start()

    order = (2, 1, 3, 0)

    def pair_copy(h, d):
        xx = (x + d) % 4
        return remote(ub.at[h, 1 - k, xx], cb.at[h, xx], cs.at[h, d], cr.at[h, d], core)

    def sum_copy(h, d):
        return remote(vb.at[h, d - 1], rb.at[h, d - 1], rs.at[h, d - 1], rr.at[h, d - 1], ring[d])

    def store(h):
        return pltpu.make_async_copy(bk.at[pl.ds(h * 512, 512)], sol.at[:, half(h)], store_sem.at[h])

    def apply(h):
        store(h).start()
        for i in range(2):
            rows = pl.ds(i * 256, 256)
            yv[h, rows, :HALF], yv[h, rows, HALF:] = split(bk[pl.ds(h * 512 + i * 256, 256), :])
        for d in order:
            xx = (x + d) % 4
            rows = pl.ds(pl.multiple_of(xx * 256, 256), 256)
            u = product(ch[rows, :], cl[rows, :], yv[h])
            for zz in range(2):
                for kk in range(2):
                    at_row = (zz * 2 + kk) * 64
                    ub[h, kk, xx, zz] = u[at_row : at_row + 64]
            pair_copy(h, d).start()

    def sum_send(h):
        for d in order[:3]:
            xx = (x + d) % 4
            pair_copy(h, d).wait_recv()
            vb[h, d - 1] = ub[h, k, xx] + cb[h, xx]
            sum_copy(h, d).start()

    def z_copy(h):
        return remote(wb.at[h, 1 - zh], zb.at[h], zs.at[h], zr.at[h], far)

    def sum_finish(h):
        pair_copy(h, 0).wait_recv()
        own = ub[h, k, x] + cb[h, x]
        for d in (1, 3, 2):
            sum_copy(h, d).wait_recv()
        wb[h] = own + (rb[h, 0] + rb[h, 1] + rb[h, 2])

        @pl.when(is_child)
        def _():
            to_parent(h, s).start()

        z_copy(h).start()

    lag = jnp.where(depth == 3, LAGS[3], jnp.where(depth == 2, LAGS[2], jnp.where(depth == 1, LAGS[1], LAGS[0])))

    def both(i, carry):
        j = i - lag

        @pl.when(jnp.logical_and(i < CHUNKS, depth > 0))
        def _():
            forward(i)

        @pl.when(j >= 0)
        def _():
            back(j)

        @pl.when(j == PER - 1)
        def _():
            apply(0)

        @pl.when(j == SENT - 1)
        def _():
            sum_send(0)

        return carry

    lax.fori_loop(0, CHUNKS + lag, both, 0)

    apply(1)
    sum_finish(0)
    sum_send(1)
    sum_finish(1)
    for h in range(2):
        z_copy(h).wait_recv()
        ob[:, half(h)] = wb[h, zh] + zb[h]
    store_out = pltpu.make_async_copy(ob, out, store_sem.at[2])
    store_out.start()

    for h in range(2):
        z_copy(h).wait_send()

        @pl.when(is_child)
        def _():
            to_parent(h, s).wait_send()
            z0(h).wait_send()

        @pl.when(is_parent)
        def _():
            for zz in range(2):
                q_copy(h, zz).wait_send()

        for d in (1, 2, 3):
            sum_copy(h, d).wait_send()
        for d in range(4):
            pair_copy(h, d).wait_send()
        for zz in range(2):
            for d in (1, 2, 3):
                gather_copy(h, zz, d, xg.at[h, zz, x, k]).wait_send()
            for d in range(4):
                core_copy(h, zz, d, xg.at[h, zz, x, k]).wait_send()

    def drain(m, carry):
        in_copy(m).wait_send()

        @pl.when(depth > 0)
        def _():
            out_copy(m).wait_send()

        return carry

    lax.fori_loop(0, CHUNKS, drain, 0)
    store(0).wait()
    store(1).wait()
    store_out.wait()


def shards(rhs, inv_factor, coupling, pattern):
    dma = pltpu.SemaphoreType.DMA
    vmem = pltpu.VMEM
    hbm = pl.BlockSpec(memory_space=pltpu.HBM)
    solved, sent = pl.pallas_call(
        kernel,
        out_shape=(jax.ShapeDtypeStruct((512, 256), F32), jax.ShapeDtypeStruct((64, 256), F32)),
        in_specs=[
            pl.BlockSpec(memory_space=pltpu.VMEM),
            hbm,
            hbm,
            pl.BlockSpec(memory_space=pltpu.SMEM),
        ],
        out_specs=(hbm, hbm),
        scratch_shapes=[
            vmem((512, 1024), F32), vmem((1024, 512), F32),
            vmem((512, 1024), BF16), vmem((512, 1024), BF16),
            vmem((1024, 512), BF16), vmem((1024, 512), BF16),
            vmem((2, 2, 4, 2, 64, HALF), F32),
            vmem((2, 1024, 2 * HALF), BF16),
            vmem((1024, HALF), F32), vmem((1024, HALF), F32), vmem((1024, HALF), F32),
            vmem((2, 512, 2 * HALF), BF16),
            vmem((2, 2, 4, 2, 64, HALF), F32), vmem((2, 4, 2, 64, HALF), F32),
            vmem((2, 3, 2, 64, HALF), F32), vmem((2, 3, 2, 64, HALF), F32),
            vmem((2, 2, 64, HALF), F32),
            vmem((2, 3, 2, 64, HALF), F32),
            vmem((2, 2, 64, HALF), F32), vmem((2, 2, 64, HALF), F32),
            vmem((2, 64, HALF), F32), vmem((64, 256), F32),
            dma((2,)), dma((3,)), dma((2,)), dma((2,)),
            dma((2, 2, 3)), dma((2, 2, 3)), dma((2, 2, 4)), dma((2, 2, 4)),
            dma((CHUNKS,)), dma((CHUNKS,)), dma((CHUNKS,)), dma((CHUNKS,)),
            dma((2, 4)), dma((2, 4)), dma((2, 3)), dma((2, 3)),
            dma((2,)), dma((2, 3)), dma((2, 2)), dma((2, 2)), dma((2,)), dma((2,)),
        ],
        compiler_params=pltpu.CompilerParams(
            collective_id=0, has_side_effects=True, vmem_limit_bytes=67_000_000
        ),
        name="eliminate",
    )(rhs[0], inv_factor[0], coupling[0], pattern[0].T)
    return solved[None], sent[None]


def solution(mesh):
    placed = (
        P("sec", ("row", "col"), None),
        P("sec", "col", "row"),
        P("sec", "row", "col"),
        P("sec", "row", "col"),
    )
    return jax.shard_map(
        shards,
        mesh=mesh,
        in_specs=placed,
        out_specs=(P("sec", "col", None), P("sec", ("row", "col"), None)),
        check_vma=False,
    )
```

time: 160 us -> 136 us (0.85)
  Pallas kernels: 153 us -> 132 us
  local copies, waits for them, and re-layouts: 6.2 us -> 3.34 us
    pallas_call x1, Pallas kernels: 153 us -> 132 us  [shards(): pl.pallas_call(kernel, out_shape=(jax.ShapeDtypeStruct((512, 256), F32),...]
    unnamed x8 -> x2, local copies, waits for them, and re-layouts: 5.44 us -> 3.34 us
where the time goes in v2:
time: 136 us
  Pallas kernels  132 us (97%)
  local copies, waits for them, and re-layouts  3.34 us (2%)
    pallas_call x1, Pallas kernels, shards(): pl.pallas_call(kernel, out_shape=(jax.ShapeDtypeStruct((512, 256), F32),...  132 us
    unnamed x2, local copies, waits for them, and re-layouts  3.34 us

profile of v2, /device:TPU:24, one launch (start us, length us, event | category | flops | bytes accessed | tf_op | source)
XLA Modules:
  0.0 136.1 jit_solution(918088086188013865)
XLA Ops:
  0.6 132.1 %eliminate.1 = (f32[512,256]{1,0:T(8,128)}, f32[64,256]{1,0:T(8,128)}) custom-call(f32[64,256]{1,0:T(8,128)} %bitcast.11, f32[512,1024]{1,0:T(8,128)} %bitcast.8, f32[1024,512]{1,0:T(8,128)} %bitcast.9, s32[4,8]{1,0:T(4,128)} %bitcast.13), custom_call_target="tpu_custom_call" | custom-call | tf_op jit(solution)/shard_map/eliminate/pallas_call | solution.py:368
  132.7 1.9 %copy.8 = f32[1,512,256]{2,1,0:T(8,128)} copy(f32[1,512,256]{2,1,0:T(8,128)} %bitcast.10) | data formatting | bytes 1048576
  134.6 1.5 %copy.9 = f32[1,64,256]{2,1,0:T(8,128)} copy(f32[1,64,256]{2,1,0:T(8,128)} %bitcast.12) | data formatting | bytes 131072

commit v3 on v2

--- a/solution.py
+++ b/solution.py
@@ -12,8 +12,8 @@
 CHUNK = 32
 PER = 512 // CHUNK
 CHUNKS = 2 * PER
+SENT = PER + 8
 LAGS = (0, CHUNKS, (3 * CHUNKS) // 4, CHUNKS // 4)
-SENT = PER + PER // 2
 
 
 def split(v):
@@ -28,8 +28,8 @@
 
 
 def kernel(
-    rhs, inv_hbm, cpl_hbm, pat, sol, out,
-    inv_v, cpl_v, ah, al, ch, cl, xg, xs, part, inb, bk, yv,
+    rhs_hbm, inv_hbm, cpl_hbm, pat_hbm, sol, out,
+    pat, rhs, inv_v, cpl_v, ah, al, ch, cl, xg, xs, part, inb, bk, yv,
     ub, cb, vb, rb, wb, pb, qb, qr, zb, ob,
     load_sem, store_sem, z0s, z0r, axs, axr, acs, acr, fs, fr, bs, br,
     cs, cr, rs, rr, ys, yr, qs, qrs, zs, zr,
@@ -54,31 +54,87 @@
             src_ref=src, dst_ref=dst, send_sem=send, recv_sem=recv, device_id=device, device_id_type=MESH
         )
 
+    load_rhs = pltpu.make_async_copy(rhs_hbm, rhs, load_sem.at[2])
+    load_pat = pltpu.make_async_copy(pat_hbm, pat, load_sem.at[3])
     load_inv = pltpu.make_async_copy(inv_hbm, inv_v, load_sem.at[0])
     load_cpl = pltpu.make_async_copy(cpl_hbm, cpl_v, load_sem.at[1])
+    barrier = pltpu.get_barrier_semaphore()
+
+    def greet(device):
+        pl.semaphore_signal(barrier, inc=1, device_id=device, device_id_type=MESH)
+
+    for device in (far, ring[2], ring[1], ring[3], {"row": inward}, core):
+        greet(device)
+
+    @pl.when(depth > 0)
+    def _():
+        greet({"row": outward})
+
+    @pl.when(is_parent)
+    def _():
+        for child in range(3):
+            greet({"sec": child})
+
+    @pl.when(is_child)
+    def _():
+        greet({"sec": 3})
+
+    load_rhs.start()
+    load_pat.start()
     load_inv.start()
     load_cpl.start()
-
-    barrier = pltpu.get_barrier_semaphore()
-
-    def greet(device):
-        pl.semaphore_signal(barrier, inc=1, device_id=device, device_id_type=MESH)
-
-    for device in (far, ring[2], ring[1], ring[3], {"row": inward}, core):
-        greet(device)
-
-    @pl.when(depth > 0)
-    def _():
-        greet({"row": outward})
-
-    @pl.when(is_parent)
-    def _():
+    load_rhs.wait()
+    pl.semaphore_wait(barrier, 7 + jnp.where(depth > 0, 1, 0) + jnp.where(is_parent, 2, 0))
+
+    def half(h):
+        return pl.ds(h * HALF, HALF)
+
+    def gather_copy(h, zz, d, src):
+        return remote(src, xg.at[h, zz, x, k], axs.at[h, zz, d - 1], axr.at[h, zz, d - 1], ring[d])
+
+    def core_copy(h, zz, d, src):
+        return remote(src, xg.at[h, zz, (x + 4 - d) % 4, k], acs.at[h, zz, d], acr.at[h, zz, d], core)
+
+    def gather_send(h, zz, src):
+        for d in (2, 1, 3):
+            gather_copy(h, zz, d, src).start()
+        core_copy(h, zz, 0, src).start()
+
+    def gather_forward(h, zz):
+        for d in (1, 3, 2):
+            piece = xg.at[h, zz, (x + 4 - d) % 4, k]
+            gather_copy(h, zz, d, piece).wait_recv()
+            core_copy(h, zz, d, piece).start()
+
+    def z0(h):
+        return remote(rhs.at[:, half(h)], xg.at[h, zh, x, k], z0s.at[h], z0r.at[h], far)
+
+    def to_parent(h, slot):
+        return remote(wb.at[h], pb.at[h, slot], ys.at[h], yr.at[h, slot], {"sec": 3})
+
+    def q_copy(h, zz):
+        return remote(qb.at[h, zz], qr.at[h, zz], qs.at[h, zz], qrs.at[h, zz], far)
+
+    def q_send(h):
         for child in range(3):
-            greet({"sec": child})
+            to_parent(h, child).wait_recv()
+        for zz in range(2):
+            mine = jnp.where(zh == zz, rhs[:, half(h)], 0.0)
+            qb[h, zz] = mine - (pb[h, 0, zz] + pb[h, 1, zz] + pb[h, 2, zz])
+            q_copy(h, zz).start()
+
+    def q_arrive(h, zz):
+        q_copy(h, zz).wait_recv()
+        xg[h, zz, x, k] = qb[h, zz] + qr[h, zz]
+        gather_send(h, zz, xg.at[h, zz, x, k])
 
     @pl.when(is_child)
     def _():
-        greet({"sec": 3})
+        for h in range(2):
+            z0(h).start()
+        for h in range(2):
+            gather_send(h, zh, rhs.at[:, half(h)])
+            xg[h, zh, x, k] = rhs[:, half(h)]
 
     load_inv.wait()
 
@@ -89,6 +145,7 @@
 
     lax.fori_loop(0, 8, split_inv, 0)
     load_cpl.wait()
+    load_pat.wait()
 
     def split_cpl(i, carry):
         rows = pl.ds(pl.multiple_of(i * 128, 128), 128)
@@ -100,57 +157,8 @@
 
     lax.fori_loop(0, 8, split_cpl, 0)
 
-    pl.semaphore_wait(barrier, 7 + jnp.where(depth > 0, 1, 0) + jnp.where(is_parent, 2, 0))
-
-    def half(h):
-        return pl.ds(h * HALF, HALF)
-
-    def gather_copy(h, zz, d, src):
-        return remote(src, xg.at[h, zz, x, k], axs.at[h, zz, d - 1], axr.at[h, zz, d - 1], ring[d])
-
-    def core_copy(h, zz, d, src):
-        return remote(src, xg.at[h, zz, (x + 4 - d) % 4, k], acs.at[h, zz, d], acr.at[h, zz, d], core)
-
-    def gather_send(h, zz, src):
-        for d in (2, 1, 3):
-            gather_copy(h, zz, d, src).start()
-        core_copy(h, zz, 0, src).start()
-
-    def gather_forward(h, zz):
-        for d in (1, 3, 2):
-            piece = xg.at[h, zz, (x + 4 - d) % 4, k]
-            gather_copy(h, zz, d, piece).wait_recv()
-            core_copy(h, zz, d, piece).start()
-
-    def z0(h):
-        return remote(rhs.at[:, half(h)], xg.at[h, zh, x, k], z0s.at[h], z0r.at[h], far)
-
-    def to_parent(h, slot):
-        return remote(wb.at[h], pb.at[h, slot], ys.at[h], yr.at[h, slot], {"sec": 3})
-
-    def q_copy(h, zz):
-        return remote(qb.at[h, zz], qr.at[h, zz], qs.at[h, zz], qrs.at[h, zz], far)
-
-    def q_send(h):
-        for child in range(3):
-            to_parent(h, child).wait_recv()
-        for zz in range(2):
-            mine = jnp.where(zh == zz, rhs[:, half(h)], 0.0)
-            qb[h, zz] = mine - (pb[h, 0, zz] + pb[h, 1, zz] + pb[h, 2, zz])
-            q_copy(h, zz).start()
-
-    def q_arrive(h, zz):
-        q_copy(h, zz).wait_recv()
-        xg[h, zz, x, k] = qb[h, zz] + qr[h, zz]
-        gather_send(h, zz, xg.at[h, zz, x, k])
-
     @pl.when(is_child)
     def _():
-        for h in range(2):
-            z0(h).start()
-        for h in range(2):
-            gather_send(h, zh, rhs.at[:, half(h)])
-            xg[h, zh, x, k] = rhs[:, half(h)]
         for h in range(2):
             gather_forward(h, zh)
         for h in range(2):
@@ -164,9 +172,9 @@
         q_send(1)
         q_arrive(0, 0)
         q_arrive(0, 1)
-        q_arrive(1, 0)
         gather_forward(0, 0)
         gather_forward(0, 1)
+        q_arrive(1, 0)
 
     def rows_of(m):
         return pl.ds(pl.multiple_of(m * CHUNK, CHUNK), CHUNK)
@@ -361,6 +369,20 @@
     store_out.wait()
 
 
+def pass_on(solved_hbm, sent_hbm, sol, out, solved, sent, in_sem, out_sem):
+    parts = [(solved_hbm.at[pl.ds(i * 128, 128)], solved.at[pl.ds(i * 128, 128)], sol.at[pl.ds(i * 128, 128)]) for i in range(4)]
+    parts.append((sent_hbm, sent, out))
+    reads = [pltpu.make_async_copy(a, b, in_sem.at[i]) for i, (a, b, _) in enumerate(parts)]
+    writes = [pltpu.make_async_copy(b, d, out_sem.at[i]) for i, (_, b, d) in enumerate(parts)]
+    for read in reads:
+        read.start()
+    for read, write in zip(reads, writes):
+        read.wait()
+        write.start()
+    for write in writes:
+        write.wait()
+
+
 def shards(rhs, inv_factor, coupling, pattern):
     dma = pltpu.SemaphoreType.DMA
     vmem = pltpu.VMEM
@@ -369,14 +391,15 @@
         kernel,
         out_shape=(jax.ShapeDtypeStruct((512, 256), F32), jax.ShapeDtypeStruct((64, 256), F32)),
         in_specs=[
-            pl.BlockSpec(memory_space=pltpu.VMEM),
             hbm,
             hbm,
-            pl.BlockSpec(memory_space=pltpu.SMEM),
+            hbm,
+            hbm,
         ],
         out_specs=(hbm, hbm),
         scratch_shapes=[
-            vmem((512, 1024), F32), vmem((1024, 512), F32),
+            pltpu.SMEM((4, 8), jnp.int32),
+            vmem((64, 256), F32), vmem((512, 1024), F32), vmem((1024, 512), F32),
             vmem((512, 1024), BF16), vmem((512, 1024), BF16),
             vmem((1024, 512), BF16), vmem((1024, 512), BF16),
             vmem((2, 2, 4, 2, 64, HALF), F32),
@@ -389,7 +412,7 @@
             vmem((2, 3, 2, 64, HALF), F32),
             vmem((2, 2, 64, HALF), F32), vmem((2, 2, 64, HALF), F32),
             vmem((2, 64, HALF), F32), vmem((64, 256), F32),
-            dma((2,)), dma((3,)), dma((2,)), dma((2,)),
+            dma((4,)), dma((3,)), dma((2,)), dma((2,)),
             dma((2, 2, 3)), dma((2, 2, 3)), dma((2, 2, 4)), dma((2, 2, 4)),
             dma((CHUNKS,)), dma((CHUNKS,)), dma((CHUNKS,)), dma((CHUNKS,)),
             dma((2, 4)), dma((2, 4)), dma((2, 3)), dma((2, 3)),
@@ -400,6 +423,15 @@
         ),
         name="eliminate",
     )(rhs[0], inv_factor[0], coupling[0], pattern[0].T)
+    solved, sent = pl.pallas_call(
+        pass_on,
+        out_shape=(jax.ShapeDtypeStruct((512, 256), F32), jax.ShapeDtypeStruct((64, 256), F32)),
+        in_specs=[hbm, hbm],
+        out_specs=(hbm, hbm),
+        scratch_shapes=[vmem((512, 256), F32), vmem((64, 256), F32), dma((5,)), dma((5,))],
+        compiler_params=pltpu.CompilerParams(vmem_limit_bytes=67_000_000),
+        name="pass_on",
+    )(solved, sent)
     return solved[None], sent[None]
 
 

time: 136 us -> 134 us (0.985)
  local copies, waits for them, and re-layouts: 3.34 us -> 0 us
  Pallas kernels: 132 us -> 134 us
    unnamed x2 -> x0, local copies, waits for them, and re-layouts: 3.34 us -> none
    pallas_call x0 -> x1, Pallas kernels: none -> 1.85 us  [shards(): pl.pallas_call(pass_on, out_shape=(jax.ShapeDtypeStruct((512, 256), F32),...]
where the time goes in v3:
time: 134 us
  Pallas kernels  134 us (100%)
    pallas_call x1, Pallas kernels, shards(): pl.pallas_call(kernel, out_shape=(jax.ShapeDtypeStruct((512, 256), F32),...  132 us

profile of v3, /device:TPU:24, one launch (start us, length us, event | category | flops | bytes accessed | tf_op | source)
XLA Modules:
  0.0 134.2 jit_solution(1523353992734520794)
XLA Ops:
  0.6 131.8 %eliminate.1 = (f32[512,256]{1,0:T(8,128)}, f32[64,256]{1,0:T(8,128)}) custom-call(f32[64,256]{1,0:T(8,128)} %bitcast.10, f32[512,1024]{1,0:T(8,128)} %bitcast.8, f32[1024,512]{1,0:T(8,128)} %bitcast.9, s32[4,8]{1,0:T(4,128)} %bitcast.11), custom_call_target="tpu_custom_call" | custom-call | tf_op jit(solution)/shard_map/eliminate/pallas_call | solution.py:390
  132.4 1.9 %pass_on.1 = (f32[512,256]{1,0:T(8,128)}, f32[64,256]{1,0:T(8,128)}) custom-call(f32[512,256]{1,0:T(8,128)} %get-tuple-element.6.solved_hbm, f32[64,256]{1,0:T(8,128)} %get-tuple-element.7.sent_hbm), custom_call_target="tpu_custom_call" | custom-call | tf_op jit(solution)/shard_map/pass_on/pallas_call | solution.py:426

commit v4 on v3

--- a/solution.py
+++ b/solution.py
@@ -13,6 +13,7 @@
 PER = 512 // CHUNK
 CHUNKS = 2 * PER
 SENT = PER + 8
+FIRST = 3
 LAGS = (0, CHUNKS, (3 * CHUNKS) // 4, CHUNKS // 4)
 
 
@@ -130,8 +131,12 @@
 
     @pl.when(is_child)
     def _():
-        for h in range(2):
-            z0(h).start()
+        z0(0).start()
+
+        @pl.when(zh == 0)
+        def _():
+            z0(1).start()
+
         for h in range(2):
             gather_send(h, zh, rhs.at[:, half(h)])
             xg[h, zh, x, k] = rhs[:, half(h)]
@@ -161,6 +166,11 @@
     def _():
         for h in range(2):
             gather_forward(h, zh)
+
+        @pl.when(zh == 1)
+        def _():
+            z0(1).start()
+
         for h in range(2):
             z0(h).wait_recv()
             gather_send(h, 1 - zh, xg.at[h, 1 - zh, x, k])
@@ -296,6 +306,7 @@
 
         z_copy(h).start()
 
+    early = depth < FIRST
     lag = jnp.where(depth == 3, LAGS[3], jnp.where(depth == 2, LAGS[2], jnp.where(depth == 1, LAGS[1], LAGS[0])))
 
     def both(i, carry):
@@ -309,11 +320,11 @@
         def _():
             back(j)
 
-        @pl.when(j == PER - 1)
+        @pl.when(jnp.logical_and(j == PER - 1, early))
         def _():
             apply(0)
 
-        @pl.when(j == SENT - 1)
+        @pl.when(jnp.logical_and(j == SENT - 1, early))
         def _():
             sum_send(0)
 
@@ -321,9 +332,23 @@
 
     lax.fori_loop(0, CHUNKS + lag, both, 0)
 
+    @pl.when(jnp.logical_not(early))
+    def _():
+        apply(0)
+
     apply(1)
+
+    @pl.when(jnp.logical_not(early))
+    def _():
+        sum_send(0)
+        sum_send(1)
+
     sum_finish(0)
-    sum_send(1)
+
+    @pl.when(early)
+    def _():
+        sum_send(1)
+
     sum_finish(1)
     for h in range(2):
         z_copy(h).wait_recv()

time: 134 us -> 132 us (0.985)
  Pallas kernels: 134 us -> 131 us
    pallas_call x1, Pallas kernels: 132 us -> 130 us  [shards(): pl.pallas_call(kernel, out_shape=(jax.ShapeDtypeStruct((512, 256), F32),...]
where the time goes in v4:
time: 132 us
  Pallas kernels  131 us (99%)
    pallas_call x1, Pallas kernels, shards(): pl.pallas_call(kernel, out_shape=(jax.ShapeDtypeStruct((512, 256), F32),...  130 us

profile of v4, /device:TPU:24, one launch (start us, length us, event | category | flops | bytes accessed | tf_op | source)
XLA Modules:
  0.0 132.1 jit_solution(16362625585792070737)
XLA Ops:
  0.6 129.6 %eliminate.1 = (f32[512,256]{1,0:T(8,128)}, f32[64,256]{1,0:T(8,128)}) custom-call(f32[64,256]{1,0:T(8,128)} %bitcast.10, f32[512,1024]{1,0:T(8,128)} %bitcast.8, f32[1024,512]{1,0:T(8,128)} %bitcast.9, s32[4,8]{1,0:T(4,128)} %bitcast.11), custom_call_target="tpu_custom_call" | custom-call | tf_op jit(solution)/shard_map/eliminate/pallas_call | solution.py:415
  130.3 1.9 %pass_on.1 = (f32[512,256]{1,0:T(8,128)}, f32[64,256]{1,0:T(8,128)}) custom-call(f32[512,256]{1,0:T(8,128)} %get-tuple-element.6.solved_hbm, f32[64,256]{1,0:T(8,128)} %get-tuple-element.7.sent_hbm), custom_call_target="tpu_custom_call" | custom-call | tf_op jit(solution)/shard_map/pass_on/pallas_call | solution.py:451

commit v5 on v4

--- a/solution.py
+++ b/solution.py
@@ -14,7 +14,7 @@
 CHUNKS = 2 * PER
 SENT = PER + 8
 FIRST = 3
-LAGS = (0, CHUNKS, (3 * CHUNKS) // 4, CHUNKS // 4)
+LAGS = (0, CHUNKS, 26, 10)
 
 
 def split(v):

time: 132 us -> 135 us (1.023)
  Pallas kernels: 131 us -> 134 us
    pallas_call x1, Pallas kernels: 130 us -> 132 us  [shards(): pl.pallas_call(kernel, out_shape=(jax.ShapeDtypeStruct((512, 256), F32),...]
where the time goes in v5:
time: 135 us
  Pallas kernels  134 us (99%)
    pallas_call x1, Pallas kernels, shards(): pl.pallas_call(kernel, out_shape=(jax.ShapeDtypeStruct((512, 256), F32),...  132 us

profile of v5, /device:TPU:24, one launch (start us, length us, event | category | flops | bytes accessed | tf_op | source)
XLA Modules:
  0.0 134.8 jit_solution(6522348227775555988)
XLA Ops:
  0.6 132.3 %eliminate.1 = (f32[512,256]{1,0:T(8,128)}, f32[64,256]{1,0:T(8,128)}) custom-call(f32[64,256]{1,0:T(8,128)} %bitcast.10, f32[512,1024]{1,0:T(8,128)} %bitcast.8, f32[1024,512]{1,0:T(8,128)} %bitcast.9, s32[4,8]{1,0:T(4,128)} %bitcast.11), custom_call_target="tpu_custom_call" | custom-call | tf_op jit(solution)/shard_map/eliminate/pallas_call | solution.py:415
  133.0 1.9 %pass_on.1 = (f32[512,256]{1,0:T(8,128)}, f32[64,256]{1,0:T(8,128)}) custom-call(f32[512,256]{1,0:T(8,128)} %get-tuple-element.6.solved_hbm, f32[64,256]{1,0:T(8,128)} %get-tuple-element.7.sent_hbm), custom_call_target="tpu_custom_call" | custom-call | tf_op jit(solution)/shard_map/pass_on/pallas_call | solution.py:451
